TPU v7x, 32 devices: a whole 2x2x4 slice. The times are simulated.
32 devices in a mesh: dp: 8 (over y, x, core), tensor: 4 (over z).
Axes of the slice: x: 2, y: 2, z: 4, core: 2. Of those that a mesh axis runs over, the one named last changes fastest.
Arguments:
- inputs: bfloat16 [2048, 2048], P(('dp', 'tensor')), parts along dimension 0, may hold values from -6 to 6
- grad_out: bfloat16 [2048, 2048], P(('dp', 'tensor')), parts along dimension 0, may hold values from -6 to 6
- gate_weight: bfloat16 [2048, 7168], P(None, 'tensor'), may hold values from -6 to 6
- up_weight: bfloat16 [2048, 7168], P(None, 'tensor'), may hold values from -6 to 6
- down_weight: bfloat16 [7168, 2048], P('tensor'), may hold values from -6 to 6
Outputs:
- grad_inputs: bfloat16 [2048, 2048], P(('dp', 'tensor')), parts along dimension 0
- grad_gate: bfloat16 [16384, 7168], P('dp', 'tensor'), parts along dimension 0
- grad_up: bfloat16 [16384, 7168], P('dp', 'tensor'), parts along dimension 0
- grad_down: bfloat16 [57344, 2048], P(('dp', 'tensor')), parts along dimension 0
There are 8 independent parts, one for each index of `dp`. A program takes and returns all parts, laid end to end along the dimension named above; an argument that names none is the same for every part. Nothing has to cross between parts.
All inputs are finite; a program needn't handle non-finite values.
Results may differ from a plain program's by a relative error of at most 0.0049.
Values may be sent and summed in bfloat16 or wider, within the bound.
A program may use at most 128 MiB of HBM per device.

v0:
```python
import jax
import jax.numpy as jnp
from jax import lax
from jax.sharding import PartitionSpec as P

D = 2048
FF = 7168


def contract_last(left, right):
    return lax.dot_general(
        left, right, (((1,), (1,)), ((), ())), preferred_element_type=jnp.float32
    )


def contract_first(left, right):
    return lax.dot_general(
        left, right, (((0,), (0,)), ((), ())), preferred_element_type=jnp.float32
    )


def on_device(inputs, grad_out, gate_weight, up_weight, down_weight):
    tokens_all = lax.all_gather(inputs, "tensor", axis=0, tiled=True)
    grads_all = lax.all_gather(grad_out, "tensor", axis=0, tiled=True)
    inv_width = D ** (-0.5)
    inv_rows = tokens_all.shape[0] ** (-0.5)
    inv_hidden = (2 * FF) ** (-0.5)
    gate = jnp.dot(tokens_all, gate_weight, preferred_element_type=jnp.float32) * inv_width
    up = jnp.dot(tokens_all, up_weight, preferred_element_type=jnp.float32) * inv_width
    sig = jax.nn.sigmoid(gate)
    act = gate * sig
    hidden = (act * up).astype(jnp.bfloat16)
    d_hidden = contract_last(grads_all, down_weight) * inv_width
    grad_down = (contract_first(hidden, grads_all) * inv_rows).astype(jnp.bfloat16)
    d_gate = (d_hidden * up * sig * (1.0 + gate * (1.0 - sig))).astype(jnp.bfloat16)
    d_up = (d_hidden * act).astype(jnp.bfloat16)
    grad_gate = (contract_first(tokens_all, d_gate) * inv_rows).astype(jnp.bfloat16)
    grad_up = (contract_first(tokens_all, d_up) * inv_rows).astype(jnp.bfloat16)
    summed = lax.psum_scatter(
        contract_last(d_gate, gate_weight) * inv_hidden
        + contract_last(d_up, up_weight) * inv_hidden,
        "tensor",
        scatter_dimension=0,
        tiled=True,
    )
    grad_inputs = summed.astype(jnp.bfloat16)
    return (grad_inputs, grad_gate, grad_up, grad_down)


def solution(mesh):
    placed = (
        P(("dp", "tensor"), None),
        P(("dp", "tensor"), None),
        P(None, "tensor"),
        P(None, "tensor"),
        P("tensor", None),
    )
    return jax.shard_map(
        on_device,
        mesh=mesh,
        in_specs=placed,
        out_specs=(
            P(("dp", "tensor"), None),
            P("dp", "tensor"),
            P("dp", "tensor"),
            P(("dp", "tensor"), None),
        ),
        check_vma=False,
    )
```

profile of v0, /device:TPU:0, one launch (start us, length us, event | category | flops | bytes accessed | tf_op | source)
XLA Modules:
  0.0 139.9 jit_solution(8619819542554499196)
XLA Ops:
  7.2 0.0 all-gather.5.cloned.1.call-start
  7.2 0.7 all-gather.5.cloned.1.call-update
  7.9 0.0 all-gather.3.cloned.1.call-start
  7.9 0.7 all-gather.3.cloned.1.call-update
  8.6 0.0 reduce-scatter.2.cloned.1.call-start
  8.7 31.5 %all-gather.5.cloned.1.call-done = bf16[256,2048]{1,0:T(8,128)(2,1)} async-done(((bf16[64,2048]{1,0:T(8,128)(2,1)}), bf16[256,2048]{1,0:T(8,128)(2,1)}) %all-gather.5.cloned.1.call-update) | async-done | bytes 1048592 | tf_op jit(solution)/shard_map/all_gather | solution.py:23
  40.2 0.0 copy-start
  40.2 6.8 %convolution_multiply_fusion = f32[256,1792]{1,0:T(8,128)} fusion(bf16[256,2048]{1,0:T(8,128)(2,1)} %all-gather.5.cloned.1.call-done, bf16[2048,1792]{1,0:T(8,128)(2,1)} %param.7), kind=kOutput, calls=%fused_computation.5 | convolution fusion | flops 1879506944 | bytes 10223616 | tf_op jit(solution)/shard_map/dot_general | solution.py:28
  47.0 0.0 copy-done
  47.0 6.6 %convolution_multiply_fusion.1 = f32[256,1792]{1,0:T(8,128)} fusion(bf16[256,2048]{1,0:T(8,128)(2,1)S(1)} %copy-done, bf16[2048,1792]{1,0:T(8,128)(2,1)} %param.8), kind=kOutput, calls=%fused_computation.6 | convolution fusion | flops 1879506944 | bytes 10223616 | tf_op jit(solution)/shard_map/dot_general | solution.py:29
  53.6 15.6 %all-gather.3.cloned.1.call-done = bf16[256,2048]{1,0:T(8,128)(2,1)} async-done(((bf16[64,2048]{1,0:T(8,128)(2,1)}), bf16[256,2048]{1,0:T(8,128)(2,1)}) %all-gather.3.cloned.1.call-update) | async-done | bytes 1048592 | tf_op jit(solution)/shard_map/all_gather | solution.py:24
  69.3 7.1 %multiply_convert_fusion.4 = (bf16[256,1792]{1,0:T(8,128)(2,1)S(1)}, bf16[256,1792]{1,0:T(8,128)(2,1)S(1)}) fusion(f32[256,1792]{1,0:T(8,128)} %convolution_multiply_fusion, f32[256,1792]{1,0:T(8,128)} %convolution_multiply_fusion.1, bf16[256,2048]{1,0:T(8,128)(2,1)} %all-gather.3.cloned.1.call-done, bf16[1792,2048]{1,0:T(8,128)(2,1)} %param.9), kind=kOutput, calls=%fused_computation.11 | convolution fusion | flops 1885470720 | bytes 13893632 | tf_op jit(solution)/shard_map/dot_general | solution.py:11
  76.3 5.2 %fusion.6 = f32[256,2048]{1,0:T(8,128)S(1)} fusion(bf16[256,1792]{1,0:T(8,128)(2,1)S(1)} %get-tuple-element.9, bf16[2048,1792]{1,0:T(8,128)(2,1)} %param.7), kind=kOutput, calls=%fused_computation.16 | convolution fusion | flops 1879048192 | bytes 10354688 | tf_op jit(solution)/shard_map/dot_general | solution.py:11
  81.5 6.6 %fusion.2 = f32[256,2048]{1,0:T(8,128)} fusion(f32[256,2048]{1,0:T(8,128)S(1)} %fusion.6, bf16[256,1792]{1,0:T(8,128)(2,1)S(1)} %get-tuple-element.8, bf16[2048,1792]{1,0:T(8,128)(2,1)} %param.8), kind=kOutput, calls=%fused_computation.9 | convolution fusion | flops 1880096768 | bytes 12451840 | tf_op jit(solution)/shard_map/dot_general | solution.py:11
  88.1 0.0 reduce-scatter.2.cloned.1.call-update
  88.1 5.2 %fusion.1 = bf16[2048,1792]{0,1:T(8,128)(2,1)} fusion(bf16[256,1792]{1,0:T(8,128)(2,1)S(1)} %get-tuple-element.8, bf16[256,2048]{1,0:T(8,128)(2,1)S(1)} %copy-done), kind=kOutput, calls=%fused_computation.4 | convolution fusion | flops 1886388224 | bytes 9306112 | tf_op jit(solution)/shard_map/dot_general | solution.py:17
  93.2 10.1 %copy.10 = bf16[2048,1792]{1,0:T(8,128)(2,1)} copy(bf16[2048,1792]{0,1:T(8,128)(2,1)} %fusion.1) | data formatting | bytes 14680064
  103.3 5.1 %fusion = bf16[2048,1792]{0,1:T(8,128)(2,1)} fusion(bf16[256,1792]{1,0:T(8,128)(2,1)S(1)} %get-tuple-element.9, bf16[256,2048]{1,0:T(8,128)(2,1)S(1)} %copy-done), kind=kOutput, calls=%fused_computation.3 | convolution fusion | flops 1886388224 | bytes 9306112 | tf_op jit(solution)/shard_map/dot_general | solution.py:17
  108.5 0.0 copy-start.1
  108.5 0.0 copy-start.2
  108.5 10.1 %copy.9 = bf16[2048,1792]{1,0:T(8,128)(2,1)} copy(bf16[2048,1792]{0,1:T(8,128)(2,1)} %fusion) | data formatting | bytes 14680064
  118.6 0.0 copy-done.1
  118.6 0.0 copy-done.2
  118.6 6.8 %multiply_convert_fusion = bf16[1792,2048]{1,0:T(8,128)(2,1)} fusion(bf16[256,2048]{1,0:T(8,128)(2,1)S(1)} %copy-done.1, f32[256,1792]{1,0:T(8,128)} %convolution_multiply_fusion.1, f32[256,1792]{1,0:T(8,128)S(1)} %copy-done.2), kind=kOutput, calls=%fused_computation | convolution fusion | flops 1889140736 | bytes 12058624 | tf_op jit(solution)/shard_map/dot_general | solution.py:17
  125.4 6.2 %reduce-scatter.2.cloned.1.call-done = f32[64,2048]{1,0:T(8,128)} async-done(((f32[256,2048]{1,0:T(8,128)}), f32[64,2048]{1,0:T(8,128)}) %reduce-scatter.2.cloned.1.call-update) | async-done | bytes 524304 | tf_op jit(solution)/shard_map/reduce_scatter | solution.py:39
  131.6 1.8 %convert_element_type.29 = bf16[64,2048]{1,0:T(8,128)(2,1)} convert(f32[64,2048]{1,0:T(8,128)} %reduce-scatter.2.cloned.1.call-done) | non-fusion elementwise | flops 131072 | bytes 786432 | tf_op jit(solution)/shard_map/convert_element_type | solution.py:46
Async XLA Ops:
  7.2 33.1 %all-gather.5.cloned.1.call-start = ((), (), s32[]{:S(2)}) async-start(), calls=%async_computation.2 | async-start | bytes 1310720 | tf_op jit(solution)/shard_map/all_gather | solution.py:23
  7.9 61.4 %all-gather.3.cloned.1.call-start = ((), (), s32[]{:S(2)}) async-start(), calls=%async_computation.1 | async-start | bytes 1310720 | tf_op jit(solution)/shard_map/all_gather | solution.py:24
  8.6 122.9 %reduce-scatter.2.cloned.1.call-start = ((), (), s32[]{:S(2)}) async-start(), calls=%async_computation.3 | async-start | bytes 2621440 | tf_op jit(solution)/shard_map/reduce_scatter | solution.py:39
  40.2 6.8 %copy-start = (bf16[256,2048]{1,0:T(8,128)(2,1)S(1)}, bf16[256,2048]{1,0:T(8,128)(2,1)}, u32[]{:S(2)}) copy-start(bf16[256,2048]{1,0:T(8,128)(2,1)} %all-gather.5.cloned.1.call-done) | copy-start | bytes 3145732
  108.5 10.1 %copy-start.1 = (bf16[256,2048]{1,0:T(8,128)(2,1)S(1)}, bf16[256,2048]{1,0:T(8,128)(2,1)}, u32[]{:S(2)}) copy-start(bf16[256,2048]{1,0:T(8,128)(2,1)} %all-gather.3.cloned.1.call-done) | copy-start | bytes 3145732
  108.5 10.1 %copy-start.2 = (f32[256,1792]{1,0:T(8,128)S(1)}, f32[256,1792]{1,0:T(8,128)}, u32[]{:S(2)}) copy-start(f32[256,1792]{1,0:T(8,128)} %convolution_multiply_fusion) | copy-start | bytes 5505028
Sparse Core Ops, SparseCore 0:
  9.6 30.6 all-gather.4
  41.8 27.4 all-gather.2
  88.2 43.3 reduce-scatter.1
where the time goes:
time: 141 us; the launch traced here: 140 us
  waiting for transfers between devices  54.7 us (39%)
  matrix products  49.3 us (35%)
  local copies, waits for them, and re-layouts  20.2 us (14%)
  between operations  13.8 us (10%)
  other arithmetic  1.77 us (1%)
    all_gather x1, waiting for transfers between devices, on_device(): tokens_all = lax.all_gather(inputs, 'tensor', axis=0, tiled=True)  31.5 us
    unnamed x8, local copies, waits for them, and re-layouts  20.2 us
    dot_general x3, matrix products, contract_last(): lax.dot_general(left, right, (((1,), (1,)), ((), ())), preferred_element_...  18.8 us
    dot_general x3, matrix products, contract_first(): lax.dot_general(left, right, (((0,), (0,)), ((), ())), preferred_element_...  17.1 us
    all_gather x1, waiting for transfers between devices, on_device(): grads_all = lax.all_gather(grad_out, 'tensor', axis=0, tiled=True)  15.6 us
    dot_general x1, matrix products, on_device(): jnp.dot(tokens_all, gate_weight, preferred_element_type=jnp.float32)  6.77 us
    dot_general x1, matrix products, on_device(): jnp.dot(tokens_all, up_weight, preferred_element_type=jnp.float32)  6.64 us
    reduce_scatter x1, waiting for transfers between devices, on_device(): lax.psum_scatter(contract_last(d_gate, gate_weight) * inv_hidden + contra...  6.19 us
  transfers between devices with their start and end apart: 3, of which 3 were waited for; matrix products, arithmetic and copies ran while one was open for 36% of the time, Pallas kernels for 0%

commit v1 on v0

--- a/solution.py
+++ b/solution.py
@@ -20,7 +20,14 @@
 
 
 def on_device(inputs, grad_out, gate_weight, up_weight, down_weight):
-    tokens_all = lax.all_gather(inputs, "tensor", axis=0, tiled=True)
+    ring = [inputs]
+    for hop in range(3):
+        ring.append(lax.ppermute(ring[-1], "tensor", [(dev, (dev + 1) % 4) for dev in range(4)]))
+    tokens_all = jnp.roll(
+        jnp.concatenate(ring[::-1], axis=0),
+        (lax.axis_index("tensor") + 1) * ring[0].shape[0],
+        axis=0,
+    )
     grads_all = lax.all_gather(grad_out, "tensor", axis=0, tiled=True)
     inv_width = D ** (-0.5)
     inv_rows = tokens_all.shape[0] ** (-0.5)

time: 141 us -> 129 us (0.915)
  local copies, waits for them, and re-layouts: 20.2 us -> 1.16 us
  waiting for transfers between devices: 54.7 us -> 62.3 us
  starting transfers between devices: 0.11 us -> 3.16 us
  matrix products: 49.3 us -> 46.5 us
    all_gather x1 -> x0, waiting for transfers between devices: 31.5 us -> none  [on_device(): tokens_all = lax.all_gather(inputs, 'tensor', axis=0, tiled=True)]
    ppermute x0 -> x3, waiting for transfers between devices: none -> 26.1 us  [on_device(): lax.ppermute(ring[-1], 'tensor', [(dev, (dev + 1) % 4) for dev in range(4)])]
    reduce_scatter x1, waiting for transfers between devices: 6.19 us -> 26.3 us  [on_device(): lax.psum_scatter(contract_last(d_gate, gate_weight) * inv_hidden + contra...]
    unnamed x8 -> x25, local copies, waits for them, and re-layouts: 20.2 us -> 1.14 us
    all_gather x1, waiting for transfers between devices: 15.6 us -> 9.89 us  [on_device(): grads_all = lax.all_gather(grad_out, 'tensor', axis=0, tiled=True)]
    dot_general x1, matrix products: 6.64 us -> 3.34 us  [on_device(): jnp.dot(tokens_all, up_weight, preferred_element_type=jnp.float32)]
    ppermute x0 -> x3, starting transfers between devices: none -> 3.08 us  [on_device(): lax.ppermute(ring[-1], 'tensor', [(dev, (dev + 1) % 4) for dev in range(4)])]
  transfers between devices with their start and end apart: 3 -> 5, of which waited for: 3 -> 5; matrix products, arithmetic and copies ran while one was open for 36% -> 22% of each run, Pallas kernels for 0% -> 0%
where the time goes in v1:
time: 129 us
  waiting for transfers between devices  62.3 us (48%)
  matrix products  46.5 us (36%)
  between operations  14.2 us (11%)
  starting transfers between devices  3.16 us (2%)
  other arithmetic  1.77 us (1%)
    reduce_scatter x1, waiting for transfers between devices, on_device(): lax.psum_scatter(contract_last(d_gate, gate_weight) * inv_hidden + contra...  26.3 us
    ppermute x3, waiting for transfers between devices, on_device(): lax.ppermute(ring[-1], 'tensor', [(dev, (dev + 1) % 4) for dev in range(4)])  26.1 us
    dot_general x3, matrix products, contract_last(): lax.dot_general(left, right, (((1,), (1,)), ((), ())), preferred_element_...  19.4 us
    dot_general x3, matrix products, contract_first(): lax.dot_general(left, right, (((0,), (0,)), ((), ())), preferred_element_...  17.2 us
    all_gather x1, waiting for transfers between devices, on_device(): grads_all = lax.all_gather(grad_out, 'tensor', axis=0, tiled=True)  9.89 us
    dot_general x1, matrix products, on_device(): jnp.dot(tokens_all, gate_weight, preferred_element_type=jnp.float32)  6.54 us
    dot_general x1, matrix products, on_device(): jnp.dot(tokens_all, up_weight, preferred_element_type=jnp.float32)  3.34 us
    ppermute x3, starting transfers between devices, on_device(): lax.ppermute(ring[-1], 'tensor', [(dev, (dev + 1) % 4) for dev in range(4)])  3.08 us
  transfers between devices with their start and end apart: 5, of which 5 were waited for; matrix products, arithmetic and copies ran while one was open for 22% of the time, Pallas kernels for 0%

profile of v1, /device:TPU:0, one launch (start us, length us, event | category | flops | bytes accessed | tf_op | source)
XLA Modules:
  0.0 129.1 jit_solution(11981346091494282228)
XLA Ops:
  7.2 0.0 copy-start
  7.2 0.0 all-gather.2.cloned.1.call-start
  7.2 3.1 %collective-permute-start = (bf16[64,2048]{1,0:T(8,128)(2,1)}, bf16[64,2048]{1,0:T(8,128)(2,1)S(1)}, u32[]{:S(2)}, u32[]{:S(2)}) collective-permute-start(bf16[64,2048]{1,0:T(8,128)(2,1)} %param.5), channel_id=1, source_target_pairs={{0,1},{1,2},{2,3},{3,0},{4,5},{5,6},{6,7},{7,4},{8,9},{9,10},{10,1... | collective-permute-start | bytes 786440 | tf_op jit(solution)/shard_map/ppermute | solution.py:25
  10.3 8.5 %collective-permute-done = bf16[64,2048]{1,0:T(8,128)(2,1)S(1)} collective-permute-done((bf16[64,2048]{1,0:T(8,128)(2,1)}, bf16[64,2048]{1,0:T(8,128)(2,1)S(1)}, u32[]{:S(2)}, u32[]{:S(2)}) %collective-permute-start) | collective-permute-done | bytes 262176 | tf_op jit(solution)/shard_map/ppermute | solution.py:25
  18.8 0.0 collective-permute-start.1
  18.8 9.3 %collective-permute-done.1 = bf16[64,2048]{1,0:T(8,128)(2,1)S(1)} collective-permute-done((bf16[64,2048]{1,0:T(8,128)(2,1)S(1)}, bf16[64,2048]{1,0:T(8,128)(2,1)S(1)}, u32[]{:S(2)}, u32[]{:S(2)}) %collective-permute-start.1) | collective-permute-done | bytes 262176 | tf_op jit(solution)/shard_map/ppermute | solution.py:25
  28.1 0.0 collective-permute-start.2
  28.1 0.0 all-gather.2.cloned.1.call-update
  28.2 0.0 reduce-scatter.2.cloned.1.call-start
  28.2 8.3 %collective-permute-done.2 = bf16[64,2048]{1,0:T(8,128)(2,1)S(1)} collective-permute-done((bf16[64,2048]{1,0:T(8,128)(2,1)S(1)}, bf16[64,2048]{1,0:T(8,128)(2,1)S(1)}, u32[]{:S(2)}, u32[]{:S(2)}) %collective-permute-start.2) | collective-permute-done | bytes 262176 | tf_op jit(solution)/shard_map/ppermute | solution.py:25
  36.6 1.0 constant_dynamic-update-slice_fusion.4
  37.6 0.0 copy-done
  37.6 0.0 slice-start
  37.7 0.0 slice-start.1
  37.7 6.5 %convolution_multiply_fusion = f32[256,1792]{1,0:T(8,128)} fusion(bf16[2048,1792]{1,0:T(8,128)(2,1)} %param.7, bf16[512,2048]{1,0:T(8,128)(2,1)S(1)} %constant_dynamic-update-slice_fusion, s32[]{:T(128)S(6)} %select_n.14), kind=kOutput, calls=%fused_computation.3 | convolution fusion | flops 1879506944 | bytes 10223620 | tf_op jit(solution)/shard_map/dot_general | solution.py:35
  44.2 0.0 slice-done
  44.2 0.0 slice-done.1
  44.2 3.3 %convolution_multiply_fusion.1 = f32[256,1792]{1,0:T(8,128)} fusion(bf16[2048,1792]{1,0:T(8,128)(2,1)S(1)} %bitcast.12, bf16[512,2048]{1,0:T(8,128)(2,1)S(1)} %constant_dynamic-update-slice_fusion, s32[]{:T(128)S(6)} %select_n.14), kind=kOutput, calls=%fused_computation.4 | convolution fusion | flops 1879506944 | bytes 10223620 | tf_op jit(solution)/shard_map/dot_general | solution.py:36
  47.6 9.9 %all-gather.2.cloned.1.call-done = bf16[256,2048]{1,0:T(8,128)(2,1)} async-done(((bf16[64,2048]{1,0:T(8,128)(2,1)}), bf16[256,2048]{1,0:T(8,128)(2,1)}) %all-gather.2.cloned.1.call-update) | async-done | bytes 1048592 | tf_op jit(solution)/shard_map/all_gather | solution.py:31
  57.5 7.0 %multiply_convert_fusion.4 = (bf16[256,1792]{1,0:T(8,128)(2,1)S(1)}, bf16[256,1792]{1,0:T(8,128)(2,1)S(1)}) fusion(f32[256,1792]{1,0:T(8,128)} %convolution_multiply_fusion, f32[256,1792]{1,0:T(8,128)} %convolution_multiply_fusion.1, bf16[256,2048]{1,0:T(8,128)(2,1)} %all-gather.2.cloned.1.call-done, bf16[1792,2048]{1,0:T(8,128)(2,1)} %param.9), kind=kOutput, calls=%fused_computation.9 | convolution fusion | flops 1885470720 | bytes 13893632 | tf_op jit(solution)/shard_map/dot_general | solution.py:11
  64.5 0.0 copy-start.3
  64.5 0.0 copy-start.2
  64.6 5.8 %fusion.12 = f32[256,2048]{1,0:T(8,128)S(1)} fusion(bf16[256,1792]{1,0:T(8,128)(2,1)S(1)} %get-tuple-element.5, bf16[2048,1792]{1,0:T(8,128)(2,1)} %param.7), kind=kOutput, calls=%fused_computation.30 | convolution fusion | flops 1879048192 | bytes 10354688 | tf_op jit(solution)/shard_map/dot_general | solution.py:11
  70.4 0.0 copy-done.3
  70.4 0.0 copy-done.2
  70.4 6.6 %fusion = f32[256,2048]{1,0:T(8,128)} fusion(f32[256,2048]{1,0:T(8,128)S(1)} %fusion.12, bf16[256,1792]{1,0:T(8,128)(2,1)S(1)} %get-tuple-element.4, bf16[2048,1792]{1,0:T(8,128)(2,1)} %param.8), kind=kOutput, calls=%fused_computation.7 | convolution fusion | flops 1880096768 | bytes 12451840 | tf_op jit(solution)/shard_map/dot_general | solution.py:11
  77.0 0.0 reduce-scatter.2.cloned.1.call-update
  77.0 0.0 copy-start.4
  77.0 6.4 %multiply_convert_fusion.1 = bf16[2048,1792]{1,0:T(8,128)(2,1)} fusion(bf16[256,1792]{1,0:T(8,128)(2,1)} %copy-done.2, bf16[512,2048]{1,0:T(8,128)(2,1)S(1)} %constant_dynamic-update-slice_fusion, s32[]{:T(128)S(6)} %select_n.14), kind=kOutput, calls=%fused_computation.1 | convolution fusion | flops 1886388224 | bytes 9306116 | tf_op jit(solution)/shard_map/dot_general | solution.py:17
  83.5 0.0 copy-done.4
  83.5 0.0 copy-start.1
  83.5 0.0 copy-start.5
  83.5 0.0 copy-start.6
  83.5 5.4 %multiply_convert_fusion.2 = bf16[2048,1792]{1,0:T(8,128)(2,1)} fusion(bf16[256,1792]{1,0:T(8,128)(2,1)S(1)} %copy-done.4, bf16[512,2048]{1,0:T(8,128)(2,1)S(1)} %constant_dynamic-update-slice_fusion, s32[]{:T(128)S(6)} %select_n.14), kind=kOutput, calls=%fused_computation.2 | convolution fusion | flops 1886388224 | bytes 9306116 | tf_op jit(solution)/shard_map/dot_general | solution.py:17
  88.9 0.0 copy-done.1
  88.9 0.0 copy-done.5
  88.9 0.0 copy-done.6
  88.9 5.4 %multiply_convert_fusion = bf16[1792,2048]{1,0:T(8,128)(2,1)} fusion(bf16[256,2048]{1,0:T(8,128)(2,1)S(1)} %copy-done.1, f32[256,1792]{1,0:T(8,128)S(1)} %copy-done.6, f32[256,1792]{1,0:T(8,128)S(1)} %copy-done.5), kind=kOutput, calls=%fused_computation | convolution fusion | flops 1889140736 | bytes 12058624 | tf_op jit(solution)/shard_map/dot_general | solution.py:17
  94.2 26.3 %reduce-scatter.2.cloned.1.call-done = f32[64,2048]{1,0:T(8,128)} async-done(((f32[256,2048]{1,0:T(8,128)}), f32[64,2048]{1,0:T(8,128)}) %reduce-scatter.2.cloned.1.call-update) | async-done | bytes 524304 | tf_op jit(solution)/shard_map/reduce_scatter | solution.py:46
  120.5 1.8 %convert_element_type.23 = bf16[64,2048]{1,0:T(8,128)(2,1)} convert(f32[64,2048]{1,0:T(8,128)} %reduce-scatter.2.cloned.1.call-done) | non-fusion elementwise | flops 131072 | bytes 786432 | tf_op jit(solution)/shard_map/convert_element_type | solution.py:53
  (8 shorter events, 0.1 us)
Async XLA Ops:
  7.2 30.5 %copy-start = (bf16[64,2048]{1,0:T(8,128)(2,1)S(1)}, bf16[64,2048]{1,0:T(8,128)(2,1)}, u32[]{:S(2)}) copy-start(bf16[64,2048]{1,0:T(8,128)(2,1)} %param.5) | copy-start | bytes 786436
  7.2 50.3 %all-gather.2.cloned.1.call-start = ((), (), s32[]{:S(2)}) async-start(), calls=%async_computation.1 | async-start | bytes 1310720 | tf_op jit(solution)/shard_map/all_gather | solution.py:31
  7.2 11.6 %collective-permute-start = (bf16[64,2048]{1,0:T(8,128)(2,1)}, bf16[64,2048]{1,0:T(8,128)(2,1)S(1)}, u32[]{:S(2)}, u32[]{:S(2)}) collective-permute-start(bf16[64,2048]{1,0:T(8,128)(2,1)} %param.5), channel_id=1, source_target_pairs={{0,1},{1,2},{2,3},{3,0},{4,5},{5,6},{6,7},{7,4},{8,9},{9,10},{10,1... | collective-permute-start | bytes 786440 | tf_op jit(solution)/shard_map/ppermute | solution.py:25
  18.8 9.3 %collective-permute-start.1 = (bf16[64,2048]{1,0:T(8,128)(2,1)S(1)}, bf16[64,2048]{1,0:T(8,128)(2,1)S(1)}, u32[]{:S(2)}, u32[]{:S(2)}) collective-permute-start(bf16[64,2048]{1,0:T(8,128)(2,1)S(1)} %collective-permute-done), channel_id=1, source_target_pairs={{0,1},{1,2},{2,3},{3,0},{4,5},{5,6},{6,7},{7,4},{8,9},{9,10},{10,1... | collective-permute-start | bytes 786440 | tf_op jit(solution)/shard_map/ppermute | solution.py:25
  28.1 8.4 %collective-permute-start.2 = (bf16[64,2048]{1,0:T(8,128)(2,1)S(1)}, bf16[64,2048]{1,0:T(8,128)(2,1)S(1)}, u32[]{:S(2)}, u32[]{:S(2)}) collective-permute-start(bf16[64,2048]{1,0:T(8,128)(2,1)S(1)} %collective-permute-done.1), channel_id=1, source_target_pairs={{0,1},{1,2},{2,3},{3,0},{4,5},{5,6},{6,7},{7,4},{8,9},{9,10},{10,1... | collective-permute-start | bytes 786440 | tf_op jit(solution)/shard_map/ppermute | solution.py:25
  28.2 92.4 %reduce-scatter.2.cloned.1.call-start = ((), (), s32[]{:S(2)}) async-start(), calls=%async_computation.2 | async-start | bytes 2621440 | tf_op jit(solution)/shard_map/reduce_scatter | solution.py:46
  37.6 6.6 %slice-start = ((s8[7340032]{0:T(1024)(128)(4,1)}), s8[4194304]{0:T(1024)(128)(4,1)S(1)}, s32[]{:S(2)}) async-start(s8[7340032]{0:T(1024)(128)(4,1)} %bitcast.11), calls=%async_computation.3 | async-start | bytes 8388608
  37.7 6.6 %slice-start.1 = ((s8[7340032]{0:T(1024)(128)(4,1)}), s8[3145728]{0:T(1024)(128)(4,1)S(1)}, s32[]{:S(2)}) async-start(s8[7340032]{0:T(1024)(128)(4,1)} %bitcast.11), calls=%async_computation.4 | async-start | bytes 6291456
  64.5 5.9 %copy-start.3 = (bf16[256,1792]{1,0:T(8,128)(2,1)}, bf16[256,1792]{1,0:T(8,128)(2,1)S(1)}, u32[]{:S(2)}) copy-start(bf16[256,1792]{1,0:T(8,128)(2,1)S(1)} %get-tuple-element.5) | copy-start | bytes 2752516
  64.5 5.9 %copy-start.2 = (bf16[256,1792]{1,0:T(8,128)(2,1)}, bf16[256,1792]{1,0:T(8,128)(2,1)S(1)}, u32[]{:S(2)}) copy-start(bf16[256,1792]{1,0:T(8,128)(2,1)S(1)} %get-tuple-element.4) | copy-start | bytes 2752516
  77.0 6.5 %copy-start.4 = (bf16[256,1792]{1,0:T(8,128)(2,1)S(1)}, bf16[256,1792]{1,0:T(8,128)(2,1)}, u32[]{:S(2)}) copy-start(bf16[256,1792]{1,0:T(8,128)(2,1)} %copy-done.3) | copy-start | bytes 2752516
  83.5 5.4 %copy-start.1 = (bf16[256,2048]{1,0:T(8,128)(2,1)S(1)}, bf16[256,2048]{1,0:T(8,128)(2,1)}, u32[]{:S(2)}) copy-start(bf16[256,2048]{1,0:T(8,128)(2,1)} %all-gather.2.cloned.1.call-done) | copy-start | bytes 3145732
  83.5 5.4 %copy-start.5 = (f32[256,1792]{1,0:T(8,128)S(1)}, f32[256,1792]{1,0:T(8,128)}, u32[]{:S(2)}) copy-start(f32[256,1792]{1,0:T(8,128)} %convolution_multiply_fusion) | copy-start | bytes 5505028
  83.5 5.4 %copy-start.6 = (f32[256,1792]{1,0:T(8,128)S(1)}, f32[256,1792]{1,0:T(8,128)}, u32[]{:S(2)}) copy-start(f32[256,1792]{1,0:T(8,128)} %convolution_multiply_fusion.1) | copy-start | bytes 5505028
Sparse Core Ops, SparseCore 0:
  28.3 29.1 all-gather.1
  77.1 43.3 reduce-scatter.1
